TPU v7x, 256 devices: a whole 4x4x8 slice. The times are simulated.
256 devices in a mesh: req: 32 (over z, y), mdl: 8 (over x, core).
Axes of the slice: x: 4, y: 4, z: 8, core: 2. Of those that a mesh axis runs over, the one named last changes fastest.
Arguments:
- stream: bfloat16 [24576, 1792], P('req'), may hold values from -6 to 6
- attention_projection_weight: bfloat16 [3, 1792, 1792], P(None, 'mdl'), may hold values from -0.125 to 0.125
- head_output_weight: bfloat16 [1792, 1792], P('mdl'), may hold values from -0.125 to 0.125
- adapter_down_maps: bfloat16 [64, 1792, 16], P('mdl'), may hold values from -0.125 to 0.125
- adapter_up_maps: bfloat16 [2, 1792, 1024], P(None, 'mdl'), may hold values from -1.5 to 1.5
- tenant_adapter_scale: float32 [4], replicated, may hold values from 0.5 to 2
- feedforward_norm_gain: bfloat16 [1792], replicated, may hold values from 0.099609375 to 1.8984375
- feedforward_weight: bfloat16 [3, 1792, 4864], P(None, 'req', 'mdl'), may hold values from -0.125 to 0.125
- prefix_cache_store: bfloat16 [1024, 2, 1792, 128], P('req', None, 'mdl'), may hold values from -140 to 140
- token_adapter_index: int32 [24576], P('req'), may hold values from 0 to 63
- request_token_lengths: int32 [32, 24], P('req'), may hold values from 1 to 192, 768 in all within a row
- request_tenant_index: int32 [768], P('req'), may hold values from 0 to 3
- last_page_holder: int32 [768, 1], replicated, may hold values from 0 to 31; in each aligned block of 24 rows (0 to 23, 24 to 47, ...) at most 2 rows name the same one
- holder_page_slot: int32 [768], replicated, may hold values from 0 to 31
- page_filled_rows: int32 [768], replicated, may hold values from 64 to 128
Outputs:
- layer_out: bfloat16 [24576, 1792], P(('req', 'mdl'))
Inputs may be any that keep to these rules, and one draw needn't show every extreme that they name: `last_page_holder`: within the rows of one index of req (aligned blocks of 24 rows) no holder is named more than 2 times, and one holder exactly 2 times in some blocks. `request_token_lengths`: each row sums to 768; its longest request has exactly 192 tokens.
All inputs are finite; a program needn't handle non-finite values.
Results may differ from a plain program's by a relative error of at most 0.025.
Values may be sent and summed in bfloat16 or wider, within the bound.
A program may use at most 128 MiB of HBM per device.

v0:
```python
import math
import jax
import jax.numpy as jnp
from jax import lax
from jax.sharding import PartitionSpec as P

HEAD_SIZE = 112
WINDOW = 64


def window_cols(one_page, fill_rows):
    return lax.dynamic_slice_in_dim(one_page, fill_rows - WINDOW, WINDOW, 2)


def per_device(
    stream,
    attention_projection_weight,
    head_output_weight,
    adapter_down_maps,
    adapter_up_maps,
    tenant_adapter_scale,
    feedforward_norm_gain,
    feedforward_weight,
    prefix_cache_store,
    token_adapter_index,
    request_token_lengths,
    request_tenant_index,
    last_page_holder,
    holder_page_slot,
    page_filled_rows,
):
    tok_count, model_width = stream.shape
    head_column_set = attention_projection_weight.shape[1]
    head_local = head_column_set // HEAD_SIZE
    req_per_dev = request_token_lengths.shape[1]
    rank_total_width = adapter_down_maps.shape[2]
    adapter_number = adapter_up_maps.shape[2] // rank_total_width
    req_devices = lax.axis_size("req")
    req_index = lax.axis_index("req")
    mdl_index = lax.axis_index("mdl")
    row_share = tok_count // lax.axis_size("mdl")
    cap_slots = max(2, (req_per_dev + req_devices - 1) // req_devices + 1)
    projected_rows = jnp.einsum(
        "td,kcd->ktc", stream, attention_projection_weight, preferred_element_type=jnp.float32
    )
    all_onehot = (
        token_adapter_index[:, None] == jnp.arange(adapter_number, dtype=jnp.int32)[None, :]
    )
    holder_count = adapter_down_maps.shape[0]
    holder_rank_rows = jnp.einsum(
        "qf,kfn->qkn", stream, adapter_down_maps, preferred_element_type=jnp.float32
    )
    held_onehot = (
        token_adapter_index[:, None]
        == (mdl_index * holder_count + jnp.arange(holder_count, dtype=jnp.int32))[None, :]
    )
    rank_part = jnp.sum(holder_rank_rows * held_onehot.astype(jnp.float32)[:, :, None], axis=1)
    rank_feat = lax.psum(rank_part.astype(jnp.bfloat16), "mdl")
    broadcast_result = (
        all_onehot.astype(jnp.bfloat16)[:, :, None] * rank_feat[:, None, :]
    ).reshape(tok_count, adapter_number * rank_total_width)
    adapter_column_set = jnp.einsum(
        "iu,pdu->ipd", broadcast_result, adapter_up_maps, preferred_element_type=jnp.float32
    )
    positions = jnp.arange(tok_count, dtype=jnp.int32)
    lengths_row = request_token_lengths[0]
    starts = jnp.cumsum(lengths_row) - lengths_row
    member = (positions[:, None] >= starts[None, :]) & (
        positions[:, None] < (starts + lengths_row)[None, :]
    )
    member_int = member.astype(jnp.int32)
    request_of = jnp.sum(member_int * jnp.arange(req_per_dev, dtype=jnp.int32)[None, :], axis=1)
    relative = positions - jnp.sum(member_int * starts[None, :], axis=1)
    tenant_hot = (
        request_tenant_index[:, None]
        == jnp.arange(tenant_adapter_scale.shape[0], dtype=jnp.int32)[None, :]
    ).astype(jnp.float32)
    request_scale = jnp.sum(tenant_hot * tenant_adapter_scale[None, :], axis=1)
    per_token_scale = jnp.sum(member.astype(jnp.float32) * request_scale[None, :], axis=1)[:, None]
    query_rows = (projected_rows[0] + per_token_scale * adapter_column_set[:, 0]).astype(
        jnp.bfloat16
    )
    key_rows = projected_rows[1].astype(jnp.bfloat16)
    value_row_block = (projected_rows[2] + per_token_scale * adapter_column_set[:, 1]).astype(
        jnp.bfloat16
    )
    owner_column = last_page_holder[:, 0]
    owner_table = owner_column.reshape(req_devices, req_per_dev)
    slot_table = holder_page_slot.reshape(req_devices, req_per_dev)
    owned = (owner_table == req_index).astype(jnp.int32)
    owned_rank = jnp.cumsum(owned, axis=1) - 1
    picked = owned[:, None, :] * (
        owned_rank[:, None, :] == jnp.arange(cap_slots, dtype=jnp.int32)[None, :, None]
    ).astype(jnp.int32)
    send_slot = jnp.sum(picked * slot_table[:, None, :], axis=2)
    my_owner = lax.dynamic_slice_in_dim(owner_column, req_index * req_per_dev, req_per_dev, 0)
    my_fill = lax.dynamic_slice_in_dim(page_filled_rows, req_index * req_per_dev, req_per_dev, 0)
    order_ids = jnp.arange(req_per_dev, dtype=jnp.int32)
    earlier = (my_owner[:, None] == my_owner[None, :]) & (order_ids[:, None] > order_ids[None, :])
    flat_pick = my_owner * cap_slots + jnp.sum(earlier.astype(jnp.int32), axis=1)
    source_pages = jnp.take(prefix_cache_store, send_slot, axis=0)
    page_inner = prefix_cache_store.shape[1:]
    arrived = lax.all_to_all(source_pages, "req", split_axis=0, concat_axis=0, tiled=True)
    chosen = jnp.take(arrived.reshape((req_devices * cap_slots,) + page_inner), flat_pick, axis=0)
    prefix_cols = jax.vmap(window_cols)(chosen, my_fill)
    prefix = jnp.transpose(prefix_cols, (0, 3, 1, 2))
    key_all = jnp.concatenate(
        [key_rows, prefix[:, :, 0].reshape(req_per_dev * WINDOW, head_column_set)], axis=0
    )
    value_all = jnp.concatenate(
        [value_row_block, prefix[:, :, 1].reshape(req_per_dev * WINDOW, head_column_set)], axis=0
    )
    distance = positions[:, None] - positions[None, :]
    local_ok = (request_of[:, None] == request_of[None, :]) & (distance >= 0) & (distance <= WINDOW)
    key_request = jnp.repeat(jnp.arange(req_per_dev, dtype=jnp.int32), WINDOW)
    key_offset = jnp.tile(jnp.arange(WINDOW, dtype=jnp.int32), req_per_dev)
    prefix_ok = (request_of[:, None] == key_request[None, :]) & (
        key_offset[None, :] >= relative[:, None]
    )
    allowed = jnp.concatenate([local_ok, prefix_ok], axis=1)
    query_heads = query_rows.reshape(tok_count, head_local, HEAD_SIZE)
    key_heads = key_all.reshape(-1, head_local, HEAD_SIZE)
    value_heads = value_all.reshape(-1, head_local, HEAD_SIZE)
    scores = jnp.einsum(
        "thd,shd->hts", query_heads, key_heads, preferred_element_type=jnp.float32
    ) * (1.0 / math.sqrt(HEAD_SIZE))
    masked = jnp.where(allowed[None], scores, -1e30)
    row_max = jnp.max(masked, axis=-1, keepdims=True)
    exp_scores = jnp.exp(masked - row_max)
    weights = (exp_scores / jnp.sum(exp_scores, axis=-1, keepdims=True)).astype(jnp.bfloat16)
    mixed = (
        jnp.einsum("hts,shd->thd", weights, value_heads, preferred_element_type=jnp.float32)
        .astype(jnp.bfloat16)
        .reshape(tok_count, head_column_set)
    )
    attn_part = (
        jnp.dot(mixed, head_output_weight, preferred_element_type=jnp.float32)
        .astype(jnp.bfloat16)
        .astype(jnp.float32)
    )
    gain_wide = feedforward_norm_gain.astype(jnp.float32)[None, :]
    attn_full = lax.psum(attn_part.astype(jnp.bfloat16), "mdl").astype(jnp.float32)
    resid_full = (stream.astype(jnp.float32) + attn_full).astype(jnp.bfloat16)
    resid_wide = resid_full.astype(jnp.float32)
    mean_sq = jnp.mean(resid_wide * resid_wide, axis=1, keepdims=True)
    normed = (resid_wide * lax.rsqrt(mean_sq + 1e-06) * gain_wide).astype(jnp.bfloat16)
    resid_mine = lax.dynamic_slice_in_dim(resid_full, mdl_index * row_share, row_share, 0)
    full_mlp = lax.all_gather(feedforward_weight, "req", axis=1, tiled=True)
    gate_part = jnp.dot(normed, full_mlp[0], preferred_element_type=jnp.float32)
    up_part = jnp.dot(normed, full_mlp[1], preferred_element_type=jnp.float32)
    hidden = (jax.nn.silu(gate_part) * up_part).astype(jnp.bfloat16)
    mlp_part = (
        jnp.einsum("tf,df->td", hidden, full_mlp[2], preferred_element_type=jnp.float32)
        .astype(jnp.bfloat16)
        .astype(jnp.float32)
    )
    mlp_mine = lax.psum_scatter(
        mlp_part.astype(jnp.bfloat16), "mdl", scatter_dimension=0, tiled=True
    ).astype(jnp.float32)
    return (resid_mine.astype(jnp.float32) + mlp_mine).astype(jnp.bfloat16)


def solution(mesh):
    return jax.shard_map(
        per_device,
        mesh=mesh,
        in_specs=(
            P("req", None),
            P(None, "mdl", None),
            P("mdl", None),
            P("mdl", None, None),
            P(None, "mdl", None),
            P(),
            P(),
            P(None, "req", "mdl"),
            P("req", None, "mdl", None),
            P("req"),
            P("req", None),
            P("req"),
            P(),
            P(),
            P(),
        ),
        out_specs=P(("req", "mdl"), None),
        check_vma=False,
    )
```

profile of v0, /device:TPU:8, one launch (start us, length us, event | category | flops | bytes accessed | tf_op | source)
XLA Modules:
  0.0 413.7 jit_solution(9208175052067111481)
XLA Ops:
  9.9 6.5 %gather_fusion = bf16[64,2,224,128]{3,2,1,0:T(8,128)(2,1)} fusion(bf16[32,2,224,128]{3,2,1,0:T(8,128)(2,1)} %param.23, s32[1024]{0:T(1024)S(1)} %pad_clamp_fusion.1), kind=kCustom, calls=%fused_computation | custom fusion | bytes 14680320 | tf_op jit(solution)/shard_map/jit(_take)/gather | solution.py:101
  16.4 6.9 %broadcast_select_fusion = bf16[32,2,2,224,128]{4,3,2,1,0:T(8,128)(2,1)} fusion(bf16[32,2,2,224,128]{4,3,2,1,0:T(8,128)(2,1)} %bitcast.74, pred[32,2]{1,0:T(8,128)(4,1)S(1)} %copy.33), kind=kLoop, calls=%fused_computation.8 | loop fusion | flops 3670016 | bytes 14680128 | tf_op jit(solution)/shard_map/jit(_take)/select_n | solution.py:101
  23.2 11.9 %all-to-all-start = ((bf16[32,2,2,224,128]{4,3,2,1,0:T(8,128)(2,1)}), bf16[32,2,2,224,128]{4,3,2,1,0:T(8,128)(2,1)}, u32[]{:S(2)}, u32[]{:S(2)}) async-start(bf16[32,2,2,224,128]{4,3,2,1,0:T(8,128)(2,1)} %broadcast_select_fusion), calls=%async_computation | async-start | bytes 14680064 | tf_op jit(solution)/shard_map/all_to_all | solution.py:103
  35.6 3.9 fusion.17
  41.0 2.8 fusion.50
  43.8 26.7 %psum.14 = bf16[768,16]{0,1:T(8,128)(2,1)S(1)} all-reduce(bf16[768,16]{0,1:T(8,128)(2,1)S(1)} %multiply_reduce_fusion), channel_id=1, replica_groups=mesh['req'=32,'mdl'=8] {'mdl'}, use_global_device_ids=true, to_apply=%region_4.5 | all-reduce | flops 12288 | bytes 49152 | tf_op jit(solution)/shard_map/psum | solution.py:58
  72.7 1.4 fusion.47
  74.1 2.1 fusion.51
  80.3 118.6 %all-to-all-done = bf16[32,2,2,224,128]{4,3,2,1,0:T(8,128)(2,1)} async-done(((bf16[32,2,2,224,128]{4,3,2,1,0:T(8,128)(2,1)}), bf16[32,2,2,224,128]{4,3,2,1,0:T(8,128)(2,1)}, u32[]{:S(2)}, u32[]{:S(2)}) %all-to-all-start) | async-done | bytes 7340064 | tf_op jit(solution)/shard_map/all_to_all | solution.py:103
  198.9 5.7 %gather_fusion.1 = bf16[24,2,224,128]{3,2,1,0:T(8,128)(2,1)} fusion(bf16[64,2,224,128]{3,2,1,0:T(8,128)(2,1)} %bitcast.16, s32[1024]{0:T(1024)S(1)} %pad_clamp_fusion), kind=kCustom, calls=%fused_computation.1 | custom fusion | bytes 5505120 | tf_op jit(solution)/shard_map/jit(_take)/gather | solution.py:104
  204.6 3.7 broadcast_select_fusion.1
  208.3 8.8 %copy.35 = bf16[24,2,224,128]{2,1,0,3:T(2,128)(2,1)} copy(bf16[24,2,224,128]{3,2,1,0:T(8,128)(2,1)} %broadcast_select_fusion.1) | data formatting | bytes 5505024 | tf_op jit(solution)/shard_map/jit(_take)/select_n | solution.py:104
  217.1 8.9 %gather_fusion.2 = bf16[24,2,224,64]{2,1,3,0:T(2,128)(2,1)S(1)} fusion(bf16[24,2,224,128]{2,1,0,3:T(2,128)(2,1)} %copy.35, s32[24]{0:T(128)S(1)} %get-tuple-element.21), kind=kCustom, calls=%fused_computation.2 | custom fusion | bytes 2752896 | tf_op jit(solution)/shard_map/vmap()/gather | solution.py:12
  226.0 6.5 %slice_reduce_fusion.1 = (bf16[24,64,224]{2,1,0:T(8,128)(2,1)S(1)}, bf16[24,64,224]{2,1,0:T(8,128)(2,1)S(1)}) fusion(bf16[24,64,2,224]{3,2,1,0:T(2,128)(2,1)S(1)} %bitcast.75), kind=kLoop, calls=%fused_computation.40 | loop fusion | bytes 2752512 | tf_op jit(solution)/shard_map/slice | solution.py:111
  234.5 9.7 %fusion.49 = (f32[2,768]{1,0:T(2,128)S(1)}, f32[2,768,2304]{2,1,0:T(8,128)}) fusion(pred[768,2304]{1,0:T(8,128)(4,1)} %pad_add_fusion, bf16[768,2,112]{0,2,1:T(8,128)(2,1)S(1)} %copy-done.6, bf16[1536,2,112]{0,2,1:T(8,128)(2,1)S(1)} %copy.37, bf16[768,2,112]{0,2,1:T(8,128)(2,1)S(1)} %bitcast.83), kind=kOutput, calls=%fused_computation.100 | convolution fusion | flops 808945920 | bytes 17307648 | tf_op jit(solution)/shard_map/sub | solution.py:129
  244.2 7.6 %fusion.22 = bf16[2,112,768]{2,1,0:T(8,128)(2,1)S(1)} fusion(f32[2,768,2304]{2,1,0:T(8,128)} %get-tuple-element.20, f32[2,768]{1,0:T(2,128)S(1)} %get-tuple-element.19, bf16[1536,2,112]{0,2,1:T(8,128)(2,1)S(1)} %copy.36, bf16[768,2,112]{0,2,1:T(8,128)(2,1)S(1)} %copy-done.5), kind=kOutput, calls=%fused_computation.41 | convolution fusion | flops 802037760 | bytes 15538176 | tf_op jit(solution)/shard_map/hts,shd->thd/dot_general | solution.py:132
  251.8 2.5 convolution_convert_fusion
  255.0 77.6 %all-reduce.3.cloned.1.call-done = bf16[768,1792]{1,0:T(8,128)(2,1)} async-done(((bf16[768,1792]{1,0:T(8,128)(2,1)}), bf16[768,1792]{1,0:T(8,128)(2,1)}) %all-reduce.3.cloned.1.call-update) | async-done | bytes 2752528 | tf_op jit(solution)/shard_map/psum | solution.py:142
  332.6 5.3 %fusion.6 = (f32[768]{0:T(1024)S(1)}, bf16[768,1792]{1,0:T(8,128)(2,1)}) fusion(bf16[768,1792]{1,0:T(8,128)(2,1)} %all-reduce.3.cloned.1.call-done, bf16[768,1792]{1,0:T(8,128)(2,1)} %param.15), kind=kLoop, calls=%fused_computation.16 | loop fusion | flops 9633024 | bytes 8260608 | tf_op jit(solution)/shard_map/reduce_sum | solution.py:145
  338.0 14.1 %all-gather.2.cloned.1.call-done = bf16[3,1792,608]{2,1,0:T(8,128)(2,1)} async-done(((bf16[3,56,608]{2,1,0:T(8,128)(2,1)}), bf16[3,1792,608]{2,1,0:T(8,128)(2,1)}) %all-gather.2.cloned.1.call-update) | async-done | bytes 6537232 | tf_op jit(solution)/shard_map/all_gather | solution.py:148
  352.0 5.8 %fusion.16 = f32[768,608]{0,1:T(8,128)} fusion(bf16[3,1792,608]{2,1,0:T(8,128)(2,1)} %all-gather.2.cloned.1.call-done, bf16[768,1792]{1,0:T(8,128)(2,1)} %get-tuple-element.10, f32[1792]{0:T(1024)S(1)} %convert_element_type.118, f32[768]{0:T(1024)S(1)} %add_rsqrt_fusion), kind=kOutput, calls=%fused_computation.35 | convolution fusion | flops 1679032320 | bytes 6924288 | tf_op jit(solution)/shard_map/dot_general | solution.py:149
  357.9 10.5 %convolution_convert_fusion.1 = bf16[768,1792]{1,0:T(8,128)(2,1)} fusion(bf16[3,1792,608]{2,1,0:T(8,128)(2,1)} %all-gather.2.cloned.1.call-done, f32[768,608]{0,1:T(8,128)} %fusion.16, bf16[768,1792]{1,0:T(8,128)(2,1)} %get-tuple-element.10, f32[1792]{0:T(1024)S(1)} %convert_element_type.118, f32[768]{0:T(1024)S(1)} %add_rsqrt_fusion), kind=kOutput, calls=%fused_computation.22 | convolution fusion | flops 3356737536 | bytes 11970560 | tf_op jit(solution)/shard_map/tf,df->td/dot_general | solution.py:153
  368.5 36.0 %reduce-scatter.2.cloned.1.call-done = bf16[96,1792]{1,0:T(8,128)(2,1)} async-done(((bf16[768,1792]{1,0:T(8,128)(2,1)}), bf16[96,1792]{1,0:T(8,128)(2,1)}) %reduce-scatter.2.cloned.1.call-update) | async-done | bytes 344080 | tf_op jit(solution)/shard_map/reduce_scatter | solution.py:157
  404.4 1.9 add_convert_fusion.1
  (78 shorter events, 13.3 us)
Async XLA Ops:
  7.4 28.2 %copy-start = (bf16[3,224,1792]{2,1,0:T(8,128)(2,1)S(1)}, bf16[3,224,1792]{2,1,0:T(8,128)(2,1)}, u32[]{:S(2)}) copy-start(bf16[3,224,1792]{2,1,0:T(8,128)(2,1)} %param.16) | copy-start | bytes 7225348
  23.2 11.9 %copy-start.9 = (s32[1,24]{1,0:T(1,128)S(1)}, s32[1,24]{1,0:T(1,128)}, u32[]{:S(2)}) copy-start(s32[1,24]{1,0:T(1,128)} %param.25) | copy-start | bytes 292
  23.2 175.7 %all-to-all-start = ((bf16[32,2,2,224,128]{4,3,2,1,0:T(8,128)(2,1)}), bf16[32,2,2,224,128]{4,3,2,1,0:T(8,128)(2,1)}, u32[]{:S(2)}, u32[]{:S(2)}) async-start(bf16[32,2,2,224,128]{4,3,2,1,0:T(8,128)(2,1)} %broadcast_select_fusion), calls=%async_computation | async-start | bytes 14680064 | tf_op jit(solution)/shard_map/all_to_all | solution.py:103
  35.1 297.5 %all-reduce.3.cloned.1.call-start = ((), (), s32[]{:S(2)}) async-start(), calls=%async_computation.2 | async-start | bytes 5505024 | tf_op jit(solution)/shard_map/psum | solution.py:142
  35.6 5.3 %copy-start.7 = (s32[768]{0:T(1024)S(1)}, s32[768]{0:T(1024)}, u32[]{:S(2)}) copy-start(s32[768]{0:T(1024)} %param.24) | copy-start | bytes 9220
  35.6 5.4 %copy-start.4 = (bf16[8,1792,16]{1,2,0:T(8,128)(2,1)S(1)}, bf16[8,1792,16]{1,2,0:T(8,128)(2,1)}, u32[]{:S(2)}) copy-start(bf16[8,1792,16]{1,2,0:T(8,128)(2,1)} %param.18) | copy-start | bytes 1376260
  39.5 1.3 copy-start.2
  40.9 31.4 %copy-start.10 = (f32[4]{0:T(128)S(1)}, f32[4]{0:T(128)}, u32[]{:S(2)}) copy-start(f32[4]{0:T(128)} %param.20) | copy-start | bytes 52
  40.9 31.4 %copy-start.11 = (s32[24]{0:T(128)S(1)}, s32[24]{0:T(128)}, u32[]{:S(2)}) copy-start(s32[24]{0:T(128)} %param.26) | copy-start | bytes 292
  232.9 1.6 copy-start.6
  234.5 9.8 %copy-start.5 = (bf16[768,2,112]{0,2,1:T(8,128)(2,1)S(1)}, bf16[768,2,112]{0,2,1:T(8,128)(2,1)}, u32[]{:S(2)}) copy-start(bf16[768,2,112]{0,2,1:T(8,128)(2,1)} %get-tuple-element.17) | copy-start | bytes 1032196
  244.2 7.6 %copy-start.3 = (bf16[224,1792]{1,0:T(8,128)(2,1)S(1)}, bf16[224,1792]{1,0:T(8,128)(2,1)}, u32[]{:S(2)}) copy-start(bf16[224,1792]{1,0:T(8,128)(2,1)} %param.17) | copy-start | bytes 2408452
  251.8 3.2 copy-start.8
  254.4 97.6 %all-gather.2.cloned.1.call-start = ((), (), s32[]{:S(2)}) async-start(), calls=%async_computation.3 | async-start | bytes 7096320 | tf_op jit(solution)/shard_map/all_gather | solution.py:148
  255.0 149.4 %reduce-scatter.2.cloned.1.call-start = ((), (), s32[]{:S(2)}) async-start(), calls=%async_computation.4 | async-start | bytes 3096576 | tf_op jit(solution)/shard_map/reduce_scatter | solution.py:157
  357.9 48.4 %copy-start.1 = (bf16[3,224,1792]{2,1,0:T(8,128)(2,1)S(1)}, bf16[3,224,1792]{2,1,0:T(8,128)(2,1)}, u32[]{:S(2)}) copy-start(bf16[3,224,1792]{2,1,0:T(8,128)(2,1)} %param.16) | copy-start | bytes 7225348
Sparse Core Ops, SparseCore 0:
  254.5 78.0 all-reduce.2
  368.6 35.7 reduce-scatter.1
Sparse Core Ops, SparseCore 1:
  257.9 94.1 all-gather.1
where the time goes:
time: 415 us; the launch traced here: 414 us
  waiting for transfers between devices  247 us (60%)
  matrix products  45 us (11%)
  local copies, waits for them, and re-layouts  42.8 us (10%)
  blocking collectives  26.7 us (6%)
  other arithmetic  25.3 us (6%)
  between operations  15.2 us (4%)
  starting transfers between devices  12 us (3%)
    all_to_all x1, waiting for transfers between devices, per_device(): lax.all_to_all(source_pages, 'req', split_axis=0, concat_axis=0, tiled=True)  119 us
    psum x1, waiting for transfers between devices, per_device(): lax.psum(attn_part.astype(jnp.bfloat16), 'mdl').astype(jnp.float32)  77.6 us
    reduce_scatter x1, waiting for transfers between devices, per_device(): lax.psum_scatter(mlp_part.astype(jnp.bfloat16), 'mdl', scatter_dimension=...  36 us
    psum x1, blocking collectives, per_device(): rank_feat = lax.psum(rank_part.astype(jnp.bfloat16), 'mdl')  26.7 us
    all_gather x1, waiting for transfers between devices, per_device(): full_mlp = lax.all_gather(feedforward_weight, 'req', axis=1, tiled=True)  14.1 us
    all_to_all x1, starting transfers between devices, per_device(): lax.all_to_all(source_pages, 'req', split_axis=0, concat_axis=0, tiled=True)  11.9 us
    dot_general x1, matrix products, per_device(): jnp.einsum('tf,df->td', hidden, full_mlp[2], preferred_element_type=jnp.f...  10.5 us
    sub x1, matrix products, per_device(): exp_scores = jnp.exp(masked - row_max)  9.74 us
  transfers between devices with their start and end apart: 4, of which 4 were waited for; matrix products, arithmetic and copies ran while one was open for 5% of the time, Pallas kernels for 0%

commit v1 on v0

--- a/solution.py
+++ b/solution.py
@@ -139,7 +139,9 @@
         .astype(jnp.float32)
     )
     gain_wide = feedforward_norm_gain.astype(jnp.float32)[None, :]
-    attn_full = lax.psum(attn_part.astype(jnp.bfloat16), "mdl").astype(jnp.float32)
+    attn_full = jnp.sum(lax.all_gather(attn_part.astype(jnp.bfloat16), "mdl"), axis=0).astype(
+        jnp.float32
+    )
     resid_full = (stream.astype(jnp.float32) + attn_full).astype(jnp.bfloat16)
     resid_wide = resid_full.astype(jnp.float32)
     mean_sq = jnp.mean(resid_wide * resid_wide, axis=1, keepdims=True)

time: 415 us -> 523 us (1.26)
  waiting for transfers between devices: 247 us -> 343 us
  other arithmetic: 25.3 us -> 39.2 us
    all_gather x0 -> x1, waiting for transfers between devices: none -> 113 us  [per_device(): lax.all_gather(attn_part.astype(jnp.bfloat16), 'mdl')]
    psum x1 -> x0, waiting for transfers between devices: 77.6 us -> none  [per_device(): lax.psum(attn_part.astype(jnp.bfloat16), 'mdl').astype(jnp.float32)]
    all_gather x1, waiting for transfers between devices: 14.1 us -> 74.3 us  [per_device(): full_mlp = lax.all_gather(feedforward_weight, 'req', axis=1, tiled=True)]
    reduce_sum x0 -> x1, other arithmetic: none -> 14 us  [per_device(): jnp.sum(lax.all_gather(attn_part.astype(jnp.bfloat16), 'mdl'), axis=0)]
  transfers between devices with their start and end apart: 4 -> 4, of which waited for: 4 -> 4; matrix products, arithmetic and copies ran while one was open for 5% -> 7% of each run, Pallas kernels for 0% -> 0%
where the time goes in v1:
time: 523 us; the launch traced here: 522 us
  waiting for transfers between devices  343 us (66%)
  matrix products  44.9 us (9%)
  local copies, waits for them, and re-layouts  42.8 us (8%)
  other arithmetic  39.2 us (7%)
  blocking collectives  26.7 us (5%)
  between operations  13.5 us (3%)
  starting transfers between devices  12 us (2%)
    all_to_all x1, waiting for transfers between devices, per_device(): lax.all_to_all(source_pages, 'req', split_axis=0, concat_axis=0, tiled=True)  119 us
    all_gather x1, waiting for transfers between devices, per_device(): lax.all_gather(attn_part.astype(jnp.bfloat16), 'mdl')  113 us
    all_gather x1, waiting for transfers between devices, per_device(): full_mlp = lax.all_gather(feedforward_weight, 'req', axis=1, tiled=True)  74.3 us
    reduce_scatter x1, waiting for transfers between devices, per_device(): lax.psum_scatter(mlp_part.astype(jnp.bfloat16), 'mdl', scatter_dimension=...  36.2 us
    psum x1, blocking collectives, per_device(): rank_feat = lax.psum(rank_part.astype(jnp.bfloat16), 'mdl')  26.7 us
    reduce_sum x1, other arithmetic, per_device(): jnp.sum(lax.all_gather(attn_part.astype(jnp.bfloat16), 'mdl'), axis=0)  14 us
    all_to_all x1, starting transfers between devices, per_device(): lax.all_to_all(source_pages, 'req', split_axis=0, concat_axis=0, tiled=True)  11.9 us
    dot_general x1, matrix products, per_device(): jnp.einsum('tf,df->td', hidden, full_mlp[2], preferred_element_type=jnp.f...  10.6 us
  transfers between devices with their start and end apart: 4, of which 4 were waited for; matrix products, arithmetic and copies ran while one was open for 7% of the time, Pallas kernels for 0%

profile of v1, /device:TPU:8, one launch (start us, length us, event | category | flops | bytes accessed | tf_op | source)
XLA Modules:
  0.0 521.9 jit_solution(5590706551452549553)
XLA Ops:
  9.0 6.5 %gather_fusion = bf16[64,2,224,128]{3,2,1,0:T(8,128)(2,1)} fusion(bf16[32,2,224,128]{3,2,1,0:T(8,128)(2,1)} %param.23, s32[1024]{0:T(1024)S(1)} %pad_clamp_fusion.1), kind=kCustom, calls=%fused_computation | custom fusion | bytes 14680320 | tf_op jit(solution)/shard_map/jit(_take)/gather | solution.py:101
  15.5 6.9 %broadcast_select_fusion = bf16[32,2,2,224,128]{4,3,2,1,0:T(8,128)(2,1)} fusion(bf16[32,2,2,224,128]{4,3,2,1,0:T(8,128)(2,1)} %bitcast.75, pred[32,2]{1,0:T(8,128)(4,1)S(1)} %copy.33), kind=kLoop, calls=%fused_computation.8 | loop fusion | flops 3670016 | bytes 14680128 | tf_op jit(solution)/shard_map/jit(_take)/select_n | solution.py:101
  22.4 11.9 %all-to-all-start = ((bf16[32,2,2,224,128]{4,3,2,1,0:T(8,128)(2,1)}), bf16[32,2,2,224,128]{4,3,2,1,0:T(8,128)(2,1)}, u32[]{:S(2)}, u32[]{:S(2)}) async-start(bf16[32,2,2,224,128]{4,3,2,1,0:T(8,128)(2,1)} %broadcast_select_fusion), calls=%async_computation | async-start | bytes 14680064 | tf_op jit(solution)/shard_map/all_to_all | solution.py:103
  34.8 3.9 fusion.17
  40.2 2.8 fusion.50
  43.0 26.7 %psum.7 = bf16[768,16]{0,1:T(8,128)(2,1)S(1)} all-reduce(bf16[768,16]{0,1:T(8,128)(2,1)S(1)} %multiply_reduce_fusion), channel_id=1, replica_groups=mesh['req'=32,'mdl'=8] {'mdl'}, use_global_device_ids=true, to_apply=%region_4.5 | all-reduce | flops 12288 | bytes 49152 | tf_op jit(solution)/shard_map/psum | solution.py:58
  73.3 2.1 fusion.51
  79.5 118.6 %all-to-all-done = bf16[32,2,2,224,128]{4,3,2,1,0:T(8,128)(2,1)} async-done(((bf16[32,2,2,224,128]{4,3,2,1,0:T(8,128)(2,1)}), bf16[32,2,2,224,128]{4,3,2,1,0:T(8,128)(2,1)}, u32[]{:S(2)}, u32[]{:S(2)}) %all-to-all-start) | async-done | bytes 7340064 | tf_op jit(solution)/shard_map/all_to_all | solution.py:103
  198.1 5.7 %gather_fusion.1 = bf16[24,2,224,128]{3,2,1,0:T(8,128)(2,1)} fusion(bf16[64,2,224,128]{3,2,1,0:T(8,128)(2,1)} %bitcast.16, s32[1024]{0:T(1024)S(1)} %pad_clamp_fusion), kind=kCustom, calls=%fused_computation.1 | custom fusion | bytes 5505120 | tf_op jit(solution)/shard_map/jit(_take)/gather | solution.py:104
  203.8 3.7 broadcast_select_fusion.1
  207.5 8.8 %copy.35 = bf16[24,2,224,128]{2,1,0,3:T(2,128)(2,1)} copy(bf16[24,2,224,128]{3,2,1,0:T(8,128)(2,1)} %broadcast_select_fusion.1) | data formatting | bytes 5505024 | tf_op jit(solution)/shard_map/jit(_take)/select_n | solution.py:104
  216.2 8.9 %gather_fusion.2 = bf16[24,2,224,64]{2,1,3,0:T(2,128)(2,1)S(1)} fusion(bf16[24,2,224,128]{2,1,0,3:T(2,128)(2,1)} %copy.35, s32[24]{0:T(128)S(1)} %get-tuple-element.21), kind=kCustom, calls=%fused_computation.2 | custom fusion | bytes 2752896 | tf_op jit(solution)/shard_map/vmap()/gather | solution.py:12
  225.1 6.5 %slice_reduce_fusion.1 = (bf16[24,64,224]{2,1,0:T(8,128)(2,1)S(1)}, bf16[24,64,224]{2,1,0:T(8,128)(2,1)S(1)}) fusion(bf16[24,64,2,224]{3,2,1,0:T(2,128)(2,1)S(1)} %bitcast.76), kind=kLoop, calls=%fused_computation.40 | loop fusion | bytes 2752512 | tf_op jit(solution)/shard_map/slice | solution.py:111
  233.7 9.7 %fusion.49 = (f32[2,768]{1,0:T(2,128)S(1)}, f32[2,768,2304]{2,1,0:T(8,128)}) fusion(pred[768,2304]{1,0:T(8,128)(4,1)} %pad_add_fusion, bf16[768,2,112]{0,2,1:T(8,128)(2,1)S(1)} %copy-done.6, bf16[1536,2,112]{0,2,1:T(8,128)(2,1)S(1)} %copy.37, bf16[768,2,112]{0,2,1:T(8,128)(2,1)S(1)} %bitcast.85), kind=kOutput, calls=%fused_computation.100 | convolution fusion | flops 808945920 | bytes 17307648 | tf_op jit(solution)/shard_map/sub | solution.py:129
  243.4 7.6 %fusion.22 = bf16[2,112,768]{2,1,0:T(8,128)(2,1)S(1)} fusion(f32[2,768,2304]{2,1,0:T(8,128)} %get-tuple-element.20, f32[2,768]{1,0:T(2,128)S(1)} %get-tuple-element.19, bf16[1536,2,112]{0,2,1:T(8,128)(2,1)S(1)} %copy.36, bf16[768,2,112]{0,2,1:T(8,128)(2,1)S(1)} %copy-done.5), kind=kOutput, calls=%fused_computation.41 | convolution fusion | flops 802037760 | bytes 15538176 | tf_op jit(solution)/shard_map/hts,shd->thd/dot_general | solution.py:132
  251.0 2.5 convolution_convert_fusion
  254.3 113.1 %all-gather.6.cloned.1.call-done = bf16[6144,1792]{1,0:T(8,128)(2,1)} async-done(((bf16[768,1792]{1,0:T(8,128)(2,1)}), bf16[6144,1792]{1,0:T(8,128)(2,1)}) %all-gather.6.cloned.1.call-update) | async-done | bytes 22020112 | tf_op jit(solution)/shard_map/all_gather | solution.py:142
  367.4 14.0 %reduce_sum.107 = bf16[768,1792]{1,0:T(8,128)(2,1)} reduce(bf16[8,768,1792]{2,1,0:T(8,128)(2,1)} %bitcast.77, bf16[]{:T(256)} %constant.87.clone.1), dimensions={0}, to_apply=%region_12.13 | reduce | flops 9633792 | bytes 24772610 | tf_op jit(solution)/shard_map/reduce_sum | solution.py:142
  381.4 5.3 %fusion.6 = (f32[768]{0:T(1024)S(1)}, bf16[768,1792]{1,0:T(8,128)(2,1)}) fusion(bf16[768,1792]{1,0:T(8,128)(2,1)} %reduce_sum.107, bf16[768,1792]{1,0:T(8,128)(2,1)} %param.15), kind=kLoop, calls=%fused_computation.16 | loop fusion | flops 9633024 | bytes 8260608 | tf_op jit(solution)/shard_map/reduce_sum | solution.py:147
  386.6 74.3 %all-gather.4.cloned.1.call-done = bf16[3,1792,608]{2,1,0:T(8,128)(2,1)} async-done(((bf16[3,56,608]{2,1,0:T(8,128)(2,1)}), bf16[3,1792,608]{2,1,0:T(8,128)(2,1)}) %all-gather.4.cloned.1.call-update) | async-done | bytes 6537232 | tf_op jit(solution)/shard_map/all_gather | solution.py:150
  460.9 5.8 %fusion.16 = f32[768,608]{0,1:T(8,128)} fusion(bf16[3,1792,608]{2,1,0:T(8,128)(2,1)} %all-gather.4.cloned.1.call-done, bf16[768,1792]{1,0:T(8,128)(2,1)} %get-tuple-element.10, f32[1792]{0:T(1024)S(1)} %convert_element_type.120, f32[768]{0:T(1024)S(1)} %add_rsqrt_fusion), kind=kOutput, calls=%fused_computation.35 | convolution fusion | flops 1679032320 | bytes 6924288 | tf_op jit(solution)/shard_map/dot_general | solution.py:151
  466.7 10.6 %convolution_convert_fusion.1 = bf16[768,1792]{1,0:T(8,128)(2,1)} fusion(bf16[3,1792,608]{2,1,0:T(8,128)(2,1)} %all-gather.4.cloned.1.call-done, f32[768,608]{0,1:T(8,128)} %fusion.16, bf16[768,1792]{1,0:T(8,128)(2,1)} %get-tuple-element.10, f32[1792]{0:T(1024)S(1)} %convert_element_type.120, f32[768]{0:T(1024)S(1)} %add_rsqrt_fusion), kind=kOutput, calls=%fused_computation.22 | convolution fusion | flops 3356737536 | bytes 11970560 | tf_op jit(solution)/shard_map/tf,df->td/dot_general | solution.py:155
  477.3 36.2 %reduce-scatter.2.cloned.1.call-done = bf16[96,1792]{1,0:T(8,128)(2,1)} async-done(((bf16[768,1792]{1,0:T(8,128)(2,1)}), bf16[96,1792]{1,0:T(8,128)(2,1)}) %reduce-scatter.2.cloned.1.call-update) | async-done | bytes 344080 | tf_op jit(solution)/shard_map/reduce_scatter | solution.py:159
  513.5 1.9 add_convert_fusion.1
  (79 shorter events, 14.8 us)
Async XLA Ops:
  6.5 28.2 %copy-start = (bf16[3,224,1792]{2,1,0:T(8,128)(2,1)S(1)}, bf16[3,224,1792]{2,1,0:T(8,128)(2,1)}, u32[]{:S(2)}) copy-start(bf16[3,224,1792]{2,1,0:T(8,128)(2,1)} %param.16) | copy-start | bytes 7225348
  22.4 11.9 %copy-start.9 = (s32[1,24]{1,0:T(1,128)S(1)}, s32[1,24]{1,0:T(1,128)}, u32[]{:S(2)}) copy-start(s32[1,24]{1,0:T(1,128)} %param.25) | copy-start | bytes 292
  22.4 175.7 %all-to-all-start = ((bf16[32,2,2,224,128]{4,3,2,1,0:T(8,128)(2,1)}), bf16[32,2,2,224,128]{4,3,2,1,0:T(8,128)(2,1)}, u32[]{:S(2)}, u32[]{:S(2)}) async-start(bf16[32,2,2,224,128]{4,3,2,1,0:T(8,128)(2,1)} %broadcast_select_fusion), calls=%async_computation | async-start | bytes 14680064 | tf_op jit(solution)/shard_map/all_to_all | solution.py:103
  34.3 333.1 %all-gather.6.cloned.1.call-start = ((), (), s32[]{:S(2)}) async-start(), calls=%async_computation.4 | async-start | bytes 24772608 | tf_op jit(solution)/shard_map/all_gather | solution.py:142
  34.8 5.3 %copy-start.7 = (s32[768]{0:T(1024)S(1)}, s32[768]{0:T(1024)}, u32[]{:S(2)}) copy-start(s32[768]{0:T(1024)} %param.24) | copy-start | bytes 9220
  34.8 5.4 %copy-start.4 = (bf16[8,1792,16]{1,2,0:T(8,128)(2,1)S(1)}, bf16[8,1792,16]{1,2,0:T(8,128)(2,1)}, u32[]{:S(2)}) copy-start(bf16[8,1792,16]{1,2,0:T(8,128)(2,1)} %param.18) | copy-start | bytes 1376260
  38.7 1.3 copy-start.2
  40.0 31.4 %copy-start.10 = (f32[4]{0:T(128)S(1)}, f32[4]{0:T(128)}, u32[]{:S(2)}) copy-start(f32[4]{0:T(128)} %param.20) | copy-start | bytes 52
  40.0 31.4 %copy-start.11 = (s32[24]{0:T(128)S(1)}, s32[24]{0:T(128)}, u32[]{:S(2)}) copy-start(s32[24]{0:T(128)} %param.26) | copy-start | bytes 292
  232.0 1.6 copy-start.6
  233.7 9.7 %copy-start.5 = (bf16[768,2,112]{0,2,1:T(8,128)(2,1)S(1)}, bf16[768,2,112]{0,2,1:T(8,128)(2,1)}, u32[]{:S(2)}) copy-start(bf16[768,2,112]{0,2,1:T(8,128)(2,1)} %get-tuple-element.17) | copy-start | bytes 1032196
  243.4 7.6 %copy-start.3 = (bf16[224,1792]{1,0:T(8,128)(2,1)S(1)}, bf16[224,1792]{1,0:T(8,128)(2,1)}, u32[]{:S(2)}) copy-start(bf16[224,1792]{1,0:T(8,128)(2,1)} %param.17) | copy-start | bytes 2408452
  251.0 3.3 copy-start.8
  253.5 207.4 %all-gather.4.cloned.1.call-start = ((), (), s32[]{:S(2)}) async-start(), calls=%async_computation.2 | async-start | bytes 7096320 | tf_op jit(solution)/shard_map/all_gather | solution.py:150
  254.3 259.2 %reduce-scatter.2.cloned.1.call-start = ((), (), s32[]{:S(2)}) async-start(), calls=%async_computation.3 | async-start | bytes 3096576 | tf_op jit(solution)/shard_map/reduce_scatter | solution.py:159
  466.7 48.7 %copy-start.1 = (bf16[3,224,1792]{2,1,0:T(8,128)(2,1)S(1)}, bf16[3,224,1792]{2,1,0:T(8,128)(2,1)}, u32[]{:S(2)}) copy-start(bf16[3,224,1792]{2,1,0:T(8,128)(2,1)} %param.16) | copy-start | bytes 7225348
Sparse Core Ops, SparseCore 0:
  253.6 113.7 all-gather.5
  370.1 90.8 all-gather.3
  477.4 36.0 reduce-scatter.1
